TPU v7x, 32 devices: a whole 2x2x4 slice. The times are simulated.
32 devices in a mesh: groups: 2 (over x), dp: 8 (over z, y), mp: 2 (over core).
Axes of the slice: x: 2, y: 2, z: 4, core: 2. Of those that a mesh axis runs over, the one named last changes fastest.
Arguments:
- residual: bfloat16 [48, 128, 8192], P(('groups', 'dp'), None, 'mp'), parts along dimension 0
- lengths: int32 [48], P(('groups', 'dp')), parts along dimension 0, may hold values from 32 to 128
- labels: int32 [48], P(('groups', 'dp')), parts along dimension 0, may hold values from 0 to 1, as said below
- earlier_means: float32 [16, 79, 2, 8192], P(('groups', 'dp'), None, None, 'mp'), parts along dimension 0
- chosen: int32 [2], P('groups'), parts along dimension 0, may hold values from 0 to 79
- norm_gain: float32 [8192], P('mp'), may hold values from 0.1 to 1.9
- key_weight: bfloat16 [2, 4096, 1024], P('mp', 'dp'), may hold values from -0.0625 to 0.0625
- value_weight: bfloat16 [2, 4096, 1024], P('mp', 'dp'), may hold values from -0.0625 to 0.0625
- out_proj: bfloat16 [2, 8192, 8192], P('groups', 'mp', 'dp'), parts along dimension 0
Outputs:
- directions: float32 [160, 8192], P('groups', 'mp'), parts along dimension 0
- key_cache: bfloat16 [48, 128, 1024], P(('groups', 'dp'), None, 'mp'), parts along dimension 0
- value_cache: bfloat16 [48, 128, 1024], P(('groups', 'dp'), None, 'mp'), parts along dimension 0
- ortho_proj: bfloat16 [2, 8192, 8192], P('groups', 'mp', 'dp'), parts along dimension 0
There are 2 independent parts, one for each index of `groups`. A program takes and returns all parts, laid end to end along the dimension named above; an argument that names none is the same for every part. Nothing has to cross between parts.
Inputs may be any that keep to these rules, and one draw needn't show every extreme that they name: Every slab of 3 consecutive prompts holds both labels.
All inputs are finite; a program needn't handle non-finite values.
Results may differ from a plain program's by a relative error of at most 0.0051.
Values may be sent and summed in bfloat16 or wider, within the bound.
A program may use at most 384 MiB of HBM per device.

v0:
```python
import math
import jax
import jax.numpy as jnp
from jax import lax
from jax.sharding import PartitionSpec as P


def direction_parts(residual, lengths, labels, earlier_means, chosen):
    highest = lax.Precision.HIGHEST
    length = residual.shape[1]
    positions = jnp.arange(length, dtype=jnp.int32)
    valid_mask = (positions[None, :] < lengths[:, None]).astype(jnp.bfloat16)
    masked_sums = jnp.einsum("pt,ptd->pd", valid_mask, residual, preferred_element_type=jnp.float32)
    prompt_mean = masked_sums / lengths.astype(jnp.float32)[:, None]
    onehot = (labels[:, None] == jnp.arange(2, dtype=jnp.int32)[None, :]).astype(jnp.float32)
    counts = jnp.sum(onehot, axis=0)
    current = jnp.sum(onehot[:, :, None] * prompt_mean[:, None, :], axis=0) / counts[:, None]
    earlier = earlier_means[0]
    layers = earlier.shape[0] + 1
    picked = lax.dynamic_index_in_dim(
        earlier, jnp.minimum(chosen[0], layers - 2), 0, keepdims=False
    )
    picked = jnp.where(chosen[0] == layers - 1, current, picked)
    weighted, totals = lax.psum((counts[:, None] * picked, counts), "dp")
    merged = weighted / totals[:, None]
    picked_difference = merged[1] - merged[0]
    share = counts / totals
    local = jnp.concatenate(
        [
            share[1] * earlier[:, 1] - share[0] * earlier[:, 0],
            (share[1] * current[1] - share[0] * current[0])[None],
        ],
        axis=0,
    )
    return (picked_difference, local)


def shards(
    residual, lengths, labels, earlier_means, chosen, norm_gain, key_weight, value_weight, out_proj
):
    highest = lax.Precision.HIGHEST
    prompts, length, half_width = residual.shape
    model_width = half_width * lax.axis_size("mp")
    picked_difference, local = direction_parts(residual, lengths, labels, earlier_means, chosen)
    key_full = lax.all_gather(key_weight, "dp", axis=1, tiled=True)[0]
    value_full = lax.all_gather(value_weight, "dp", axis=1, tiled=True)[0]
    difference = lax.psum(local, "dp")
    square_sums = lax.psum(jnp.sum(difference * difference, axis=1), "mp")
    directions = difference * lax.rsqrt(square_sums / model_width + 1e-06)[:, None]
    local_square = jnp.sum(picked_difference * picked_difference)
    local_mean = local_square / half_width + 1e-06
    unit = picked_difference * lax.rsqrt(local_mean)
    token_rows = residual.reshape(prompts * length, half_width)
    row_values = token_rows.astype(jnp.float32)
    matrix = out_proj[0]
    dots = jnp.sum(row_values * unit[None, :], axis=1)
    columns = jnp.sum(matrix.astype(jnp.float32) * unit[:, None], axis=0)
    packed = jnp.concatenate([dots, columns, local_square[None]])
    pieces = lax.all_gather(packed, "mp")
    squares = pieces[:, -1]
    mean_dir = jnp.sum(squares) / model_width + 1e-06
    ratios = jnp.sqrt((squares / half_width + 1e-06) / mean_dir) / math.sqrt(model_width)
    sums = jnp.sum(pieces * ratios[:, None], axis=0)
    projection = sums[: prompts * length]
    column_proj = sums[prompts * length : -1]
    refusal_dir = picked_difference * (lax.rsqrt(mean_dir) / math.sqrt(model_width))
    ablated = row_values - projection[:, None] * refusal_dir[None, :]
    mean_square = lax.psum(jnp.sum(ablated * ablated, axis=1), "mp") / model_width
    normed = (ablated * lax.rsqrt(mean_square + 1e-05)[:, None] * norm_gain[None, :]).astype(
        jnp.bfloat16
    )
    ortho_proj = (matrix.astype(jnp.float32) - refusal_dir[:, None] * column_proj[None, :]).astype(
        jnp.bfloat16
    )[None]
    key_sum = jnp.dot(normed, key_full, preferred_element_type=jnp.float32)
    value_sum = jnp.dot(normed, value_full, preferred_element_type=jnp.float32)
    key_sums, value_sums = (
        lax.psum_scatter(key_sum, "mp", scatter_dimension=1, tiled=True),
        lax.psum_scatter(value_sum, "mp", scatter_dimension=1, tiled=True),
    )
    key_cache = key_sums.astype(jnp.bfloat16).reshape(prompts, length, key_sums.shape[1])
    value_cache = value_sums.astype(jnp.bfloat16).reshape(prompts, length, value_sums.shape[1])
    return (directions, key_cache, value_cache, ortho_proj)


def solution(mesh):
    return jax.shard_map(
        shards,
        mesh=mesh,
        in_specs=(
            P(("groups", "dp"), None, "mp"),
            P(("groups", "dp")),
            P(("groups", "dp")),
            P(("groups", "dp"), None, None, "mp"),
            P("groups"),
            P("mp"),
            P("mp", "dp", None),
            P("mp", "dp", None),
            P("groups", "mp", "dp"),
        ),
        out_specs=(
            P("groups", "mp"),
            P(("groups", "dp"), None, "mp"),
            P(("groups", "dp"), None, "mp"),
            P("groups", "mp", "dp"),
        ),
        check_vma=False,
    )
```

profile of v0, /device:TPU:0, one launch (start us, length us, event | category | flops | bytes accessed | tf_op | source)
XLA Modules:
  0.0 425.7 jit_solution(17136357276199874435)
XLA Ops:
  7.2 0.0 all-reduce.5.cloned.1.call-start
  7.2 0.9 fusion.14
  8.1 0.7 convert_element_type.46
  8.8 0.8 fusion.15
  9.6 0.7 compare_convert_fusion
  10.9 0.1 copy.17
  11.0 4.7 %copy.24 = f32[1,79,2,4096]{3,1,2,0:T(8,128)} copy(f32[1,79,2,4096]{3,2,1,0:T(2,128)} %param.12) | data formatting | bytes 5177344 | tf_op args[3]
  15.7 0.5 fusion.12
  16.2 0.1 bitcast_divide_fusion
  16.3 0.1 multiply_reduce_fusion.2
  16.4 0.9 fusion.10
  17.3 39.2 %all-reduce.1 = (f32[2]{0:T(128)S(1)}, f32[2,4096]{1,0:T(2,128)S(1)}) all-reduce(f32[2]{0:T(128)S(1)} %fusion.15, f32[2,4096]{1,0:T(2,128)S(1)} %get-tuple-element.10), channel_id=1, replica_groups=mesh['groups'=2,'dp'=8,'mp'=2] {'dp'}, use_global_device_ids=true, to_apply=%region_1.0 | all-reduce | flops 8194 | bytes 65552 | tf_op jit(solution)/shard_map/psum | solution.py:24
  56.5 0.6 fusion.16
  57.0 1.3 fusion.11
  58.4 3.1 fusion.9
  61.5 1.2 pad_maximum_fusion
  62.7 0.0 all-reduce.5.cloned.1.call-update
  62.7 0.0 all-gather.4.cloned.1.call-start
  62.8 0.7 all-gather.4.cloned.1.call-update
  63.5 0.0 all-gather.6.cloned.1.call-start
  63.5 0.7 all-gather.6.cloned.1.call-update
  64.2 0.0 reduce-scatter.3.cloned.1.call-start
  64.3 0.1 broadcast_divide_fusion
  64.3 0.6 multiply_reduce_fusion.3
  65.7 0.6 dynamic-slice.1
  67.0 0.7 fusion.7
  67.7 5.1 %fusion.1 = f32[1024]{0:T(1024)S(1)} fusion(bf16[1,4096,1024]{2,1,0:T(8,128)(2,1)} %param.17, f32[4096]{0:T(1024)S(1)} %bitcast.54), kind=kLoop, calls=%fused_computation.3 | loop fusion | flops 12581888 | bytes 8409088 | tf_op jit(solution)/shard_map/reduce_sum | solution.py:57
  72.8 0.8 maximum_dynamic-update-slice_fusion
  73.6 3.3 all-reduce
  76.8 0.1 reshape.183
  76.9 0.6 slice_reduce_fusion
  78.2 0.1 multiply_reduce_fusion.5
  78.3 0.1 multiply_reduce_fusion.4
  78.5 1.2 multiply_reduce_fusion
  79.7 63.7 %all-reduce.5.cloned.1.call-done = f32[80,4096]{1,0:T(8,128)} async-done(((f32[80,4096]{1,0:T(8,128)}), f32[80,4096]{1,0:T(8,128)}) %all-reduce.5.cloned.1.call-update) | async-done | bytes 1310736 | tf_op jit(solution)/shard_map/psum | solution.py:47
  143.4 1.5 multiply_reduce_fusion.1
  144.9 2.5 all-reduce.2
  147.4 3.4 multiply_convert_fusion
  150.8 119.1 %all-gather.4.cloned.1.call-done = bf16[1,4096,1024]{2,1,0:T(8,128)(2,1)} async-done(((bf16[1,512,1024]{2,1,0:T(8,128)(2,1)}), bf16[1,4096,1024]{2,1,0:T(8,128)(2,1)}) %all-gather.4.cloned.1.call-update) | async-done | bytes 8388624 | tf_op jit(solution)/shard_map/all_gather | solution.py:45
  269.9 9.0 %fusion.5 = f32[384,1024]{1,0:T(8,128)} fusion(bf16[384,4096]{1,0:T(8,128)(2,1)} %bitcast.46, bf16[1,4096,1024]{2,1,0:T(8,128)(2,1)} %all-gather.4.cloned.1.call-done), kind=kOutput, calls=%fused_computation.7 | convolution fusion | flops 3221225472 | bytes 13107200 | tf_op jit(solution)/shard_map/dot_general | solution.py:75
  279.0 0.0 reduce-scatter.5.cloned.1.call-start
  279.0 116.4 %all-gather.6.cloned.1.call-done = bf16[1,4096,1024]{2,1,0:T(8,128)(2,1)} async-done(((bf16[1,512,1024]{2,1,0:T(8,128)(2,1)}), bf16[1,4096,1024]{2,1,0:T(8,128)(2,1)}) %all-gather.6.cloned.1.call-update) | async-done | bytes 8388624 | tf_op jit(solution)/shard_map/all_gather | solution.py:46
  395.4 7.0 %fusion.3 = f32[384,1024]{1,0:T(8,128)} fusion(bf16[384,4096]{1,0:T(8,128)(2,1)S(1)} %bitcast.47, bf16[1,4096,1024]{2,1,0:T(8,128)(2,1)} %all-gather.6.cloned.1.call-done), kind=kOutput, calls=%fused_computation.5 | convolution fusion | flops 3221225472 | bytes 13107200 | tf_op jit(solution)/shard_map/dot_general | solution.py:76
  402.5 8.0 %fusion.2 = bf16[1,4096,1024]{2,1,0:T(8,128)(2,1)} fusion(bf16[1,4096,1024]{2,1,0:T(8,128)(2,1)} %param.17, f32[1024]{0:T(1024)S(1)} %slice.54, f32[4096]{0:T(1024)S(1)} %bitcast.52), kind=kLoop, calls=%fused_computation.4 | loop fusion | flops 16777216 | bytes 16797696 | tf_op jit(solution)/shard_map/convert_element_type | solution.py:72
  410.5 1.2 broadcast_multiply_fusion
  411.7 1.9 convert_element_type.52
  413.7 3.6 reduce-scatter.5.cloned.1.call-done
  417.2 1.9 convert_element_type.53
  (21 shorter events, 0.1 us)
Async XLA Ops:
  7.2 8.5 %copy-start = (bf16[3,128,4096]{2,1,0:T(8,128)(2,1)S(1)}, bf16[3,128,4096]{2,1,0:T(8,128)(2,1)}, u32[]{:S(2)}) copy-start(bf16[3,128,4096]{2,1,0:T(8,128)(2,1)} %param.9) | copy-start | bytes 9437188
  7.2 136.2 %all-reduce.5.cloned.1.call-start = ((), (), s32[]{:S(2)}) async-start(), calls=%async_computation.2 | async-start | bytes 2621440 | tf_op jit(solution)/shard_map/psum | solution.py:47
  61.5 4.2 copy-start.4
  62.7 207.2 %all-gather.4.cloned.1.call-start = ((), (), s32[]{:S(2)}) async-start(), calls=%async_computation.3 | async-start | bytes 9437184 | tf_op jit(solution)/shard_map/all_gather | solution.py:45
  63.5 331.9 %all-gather.6.cloned.1.call-start = ((), (), s32[]{:S(2)}) async-start(), calls=%async_computation.5 | async-start | bytes 9437184 | tf_op jit(solution)/shard_map/all_gather | solution.py:46
  64.2 347.5 %reduce-scatter.3.cloned.1.call-start = ((), (), s32[]{:S(2)}) async-start(), calls=%async_computation.4 | async-start | bytes 2359296 | tf_op jit(solution)/shard_map/reduce_scatter | solution.py:78
  72.8 74.6 %copy-start.3 = (f32[4096]{0:T(1024)S(1)}, f32[4096]{0:T(1024)}, u32[]{:S(2)}) copy-start(f32[4096]{0:T(1024)} %param.14) | copy-start | bytes 49156
  269.9 125.5 %copy-start.2 = (bf16[3,128,4096]{2,1,0:T(8,128)(2,1)S(1)}, bf16[3,128,4096]{2,1,0:T(8,128)(2,1)}, u32[]{:S(2)}) copy-start(bf16[3,128,4096]{2,1,0:T(8,128)(2,1)} %multiply_convert_fusion) | copy-start | bytes 9437188
  279.0 138.3 %reduce-scatter.5.cloned.1.call-start = ((), (), s32[]{:S(2)}) async-start(), calls=%async_computation.6 | async-start | bytes 2359296 | tf_op jit(solution)/shard_map/reduce_scatter | solution.py:79
  402.4 8.0 %copy-start.1 = (f32[80,4096]{1,0:T(8,128)S(1)}, f32[80,4096]{1,0:T(8,128)}, u32[]{:S(2)}) copy-start(f32[80,4096]{1,0:T(8,128)} %all-reduce.5.cloned.1.call-done) | copy-start | bytes 3932164
Sparse Core Ops, SparseCore 0:
  62.8 80.5 all-reduce.4
  145.7 124.1 all-gather.3
  272.2 123.1 all-gather.5
  397.6 7.2 reduce-scatter.2
  406.9 10.2 reduce-scatter.4
where the time goes:
time: 426 us
  waiting for transfers between devices  304 us (71%)
  blocking collectives  44.9 us (11%)
  other arithmetic  37 us (9%)
  between operations  16.7 us (4%)
  matrix products  16.6 us (4%)
  local copies, waits for them, and re-layouts  6.11 us (1%)
    all_gather x1, waiting for transfers between devices, shards(): key_full = lax.all_gather(key_weight, 'dp', axis=1, tiled=True)[0]  119 us
    all_gather x1, waiting for transfers between devices, shards(): value_full = lax.all_gather(value_weight, 'dp', axis=1, tiled=True)[0]  116 us
    psum x1, waiting for transfers between devices, shards(): difference = lax.psum(local, 'dp')  63.7 us
    psum x1, blocking collectives, direction_parts(): weighted, totals = lax.psum((counts[:, None] * picked, counts), 'dp')  39.2 us
    dot_general x1, matrix products, shards(): key_sum = jnp.dot(normed, key_full, preferred_element_type=jnp.float32)  9.04 us
  transfers between devices with their start and end apart: 5, of which 4 were waited for; matrix products, arithmetic and copies ran while one was open for 10% of the time, Pallas kernels for 0%

commit v1 on v0

--- a/solution.py
+++ b/solution.py
@@ -44,7 +44,7 @@
     picked_difference, local = direction_parts(residual, lengths, labels, earlier_means, chosen)
     key_full = lax.all_gather(key_weight, "dp", axis=1, tiled=True)[0]
     value_full = lax.all_gather(value_weight, "dp", axis=1, tiled=True)[0]
-    difference = lax.psum(local, "dp")
+    difference = jnp.sum(lax.all_gather(local, "dp"), axis=0)
     square_sums = lax.psum(jnp.sum(difference * difference, axis=1), "mp")
     directions = difference * lax.rsqrt(square_sums / model_width + 1e-06)[:, None]
     local_square = jnp.sum(picked_difference * picked_difference)

time: 426 us -> 489 us (1.15)
  waiting for transfers between devices: 304 us -> 364 us
  other arithmetic: 37 us -> 42.8 us
    all_gather x0 -> x1, waiting for transfers between devices: none -> 130 us  [shards(): difference = jnp.sum(lax.all_gather(local, 'dp'), axis=0)]
    psum x1 -> x0, waiting for transfers between devices: 63.7 us -> none  [shards(): difference = lax.psum(local, 'dp')]
    all_gather x1, waiting for transfers between devices: 119 us -> 112 us  [shards(): key_full = lax.all_gather(key_weight, 'dp', axis=1, tiled=True)[0]]
    reduce_sum x0 -> x1, other arithmetic: none -> 5.87 us  [shards(): difference = jnp.sum(lax.all_gather(local, 'dp'), axis=0)]
where the time goes in v1:
time: 489 us
  waiting for transfers between devices  364 us (74%)
  blocking collectives  45.1 us (9%)
  other arithmetic  42.8 us (9%)
  matrix products  18.4 us (4%)
  between operations  16.7 us (3%)
    all_gather x1, waiting for transfers between devices, shards(): difference = jnp.sum(lax.all_gather(local, 'dp'), axis=0)  130 us
    all_gather x1, waiting for transfers between devices, shards(): value_full = lax.all_gather(value_weight, 'dp', axis=1, tiled=True)[0]  116 us
    all_gather x1, waiting for transfers between devices, shards(): key_full = lax.all_gather(key_weight, 'dp', axis=1, tiled=True)[0]  112 us
    psum x1, blocking collectives, direction_parts(): weighted, totals = lax.psum((counts[:, None] * picked, counts), 'dp')  39.2 us
  transfers between devices with their start and end apart: 5, of which 4 were waited for; matrix products, arithmetic and copies ran while one was open for 10% of the time, Pallas kernels for 0%

profile of v1, /device:TPU:0, one launch (start us, length us, event | category | flops | bytes accessed | tf_op | source)
XLA Modules:
  0.0 488.9 jit_solution(15337276349135342574)
XLA Ops:
  7.2 0.0 all-gather.10.cloned.1.call-start
  7.2 0.9 fusion.13
  8.1 0.7 convert_element_type.46
  8.8 0.8 fusion.14
  9.5 0.7 compare_convert_fusion
  10.8 0.1 copy.13
  10.9 2.4 fusion.11
  13.3 0.1 bitcast_divide_fusion
  13.4 0.1 multiply_reduce_fusion.2
  13.6 0.1 fusion.9
  13.7 39.2 %all-reduce.1 = (f32[2]{0:T(128)S(1)}, f32[2,4096]{1,0:T(2,128)S(1)}) all-reduce(f32[2]{0:T(128)S(1)} %fusion.14, f32[2,4096]{1,0:T(2,128)S(1)} %get-tuple-element.10), channel_id=1, replica_groups=mesh['groups'=2,'dp'=8,'mp'=2] {'dp'}, use_global_device_ids=true, to_apply=%region_1.0 | all-reduce | flops 8194 | bytes 65552 | tf_op jit(solution)/shard_map/psum | solution.py:24
  52.8 0.6 fusion.15
  53.4 1.3 fusion.10
  54.8 3.0 fusion.8
  57.7 0.8 copy.21
  58.6 1.2 pad_maximum_fusion
  59.8 0.0 all-gather.6.cloned.1.call-start
  59.8 0.7 all-gather.6.cloned.1.call-update
  60.5 0.0 all-gather.8.cloned.1.call-start
  60.6 0.7 all-gather.8.cloned.1.call-update
  61.3 0.0 reduce-scatter.3.cloned.1.call-start
  61.3 0.1 broadcast_divide_fusion
  61.4 0.6 multiply_reduce_fusion.3
  62.7 0.6 dynamic-slice.1
  64.0 0.7 fusion.7
  64.7 5.9 %fusion.1 = f32[1024]{0:T(1024)S(1)} fusion(bf16[1,4096,1024]{2,1,0:T(8,128)(2,1)} %param.17, f32[4096]{0:T(1024)S(1)} %bitcast.56), kind=kLoop, calls=%fused_computation.3 | loop fusion | flops 12581888 | bytes 8409088 | tf_op jit(solution)/shard_map/reduce_sum | solution.py:57
  70.7 0.8 maximum_dynamic-update-slice_fusion
  71.5 3.3 all-reduce
  74.7 0.1 reshape.184
  74.8 0.6 slice_reduce_fusion
  76.1 0.1 multiply_reduce_fusion.5
  76.2 0.1 multiply_reduce_fusion.4
  76.4 1.2 multiply_reduce_fusion
  77.6 130.5 %all-gather.10.cloned.1.call-done = f32[640,4096]{1,0:T(8,128)} async-done(((f32[80,4096]{1,0:T(8,128)}), f32[640,4096]{1,0:T(8,128)}) %all-gather.10.cloned.1.call-update) | async-done | bytes 10485776 | tf_op jit(solution)/shard_map/all_gather | solution.py:47
  208.0 5.9 %reduce_sum.96 = f32[80,4096]{1,0:T(8,128)} reduce(f32[8,80,4096]{2,1,0:T(8,128)} %bitcast.45, f32[]{:T(128)} %constant.12.clone.1), dimensions={0}, to_apply=%region_3.4 | reduce | flops 2293760 | bytes 11796484 | tf_op jit(solution)/shard_map/reduce_sum | solution.py:47
  213.9 1.5 multiply_reduce_fusion.1
  215.4 2.7 all-reduce.2
  218.1 3.4 multiply_convert_fusion
  221.5 111.9 %all-gather.6.cloned.1.call-done = bf16[1,4096,1024]{2,1,0:T(8,128)(2,1)} async-done(((bf16[1,512,1024]{2,1,0:T(8,128)(2,1)}), bf16[1,4096,1024]{2,1,0:T(8,128)(2,1)}) %all-gather.6.cloned.1.call-update) | async-done | bytes 8388624 | tf_op jit(solution)/shard_map/all_gather | solution.py:45
  333.3 9.0 %fusion.5 = f32[384,1024]{1,0:T(8,128)} fusion(bf16[384,4096]{1,0:T(8,128)(2,1)} %bitcast.47, bf16[1,4096,1024]{2,1,0:T(8,128)(2,1)} %all-gather.6.cloned.1.call-done), kind=kOutput, calls=%fused_computation.7 | convolution fusion | flops 3221225472 | bytes 13107200 | tf_op jit(solution)/shard_map/dot_general | solution.py:75
  342.4 0.0 reduce-scatter.5.cloned.1.call-start
  342.4 116.2 %all-gather.8.cloned.1.call-done = bf16[1,4096,1024]{2,1,0:T(8,128)(2,1)} async-done(((bf16[1,512,1024]{2,1,0:T(8,128)(2,1)}), bf16[1,4096,1024]{2,1,0:T(8,128)(2,1)}) %all-gather.8.cloned.1.call-update) | async-done | bytes 8388624 | tf_op jit(solution)/shard_map/all_gather | solution.py:46
  458.6 6.9 %fusion.3 = f32[384,1024]{1,0:T(8,128)} fusion(bf16[384,4096]{1,0:T(8,128)(2,1)S(1)} %bitcast.48, bf16[1,4096,1024]{2,1,0:T(8,128)(2,1)} %all-gather.8.cloned.1.call-done), kind=kOutput, calls=%fused_computation.5 | convolution fusion | flops 3221225472 | bytes 13107200 | tf_op jit(solution)/shard_map/dot_general | solution.py:76
  465.6 8.0 %fusion.2 = bf16[1,4096,1024]{2,1,0:T(8,128)(2,1)} fusion(bf16[1,4096,1024]{2,1,0:T(8,128)(2,1)} %param.17, f32[1024]{0:T(1024)S(1)} %slice.54, f32[4096]{0:T(1024)S(1)} %bitcast.54), kind=kLoop, calls=%fused_computation.4 | loop fusion | flops 16777216 | bytes 16797696 | tf_op jit(solution)/shard_map/convert_element_type | solution.py:72
  473.6 1.2 broadcast_multiply_fusion
  474.8 1.9 convert_element_type.52
  476.8 3.7 reduce-scatter.5.cloned.1.call-done
  480.4 1.9 convert_element_type.53
  (24 shorter events, 0.1 us)
Async XLA Ops:
  7.2 6.4 %copy-start.3 = (f32[1,79,2,4096]{3,2,1,0:T(2,128)S(1)}, f32[1,79,2,4096]{3,2,1,0:T(2,128)}, u32[]{:S(2)}) copy-start(f32[1,79,2,4096]{3,2,1,0:T(2,128)} %param.12) | copy-start | bytes 7766020
  7.2 200.9 %all-gather.10.cloned.1.call-start = ((), (), s32[]{:S(2)}) async-start(), calls=%async_computation.6 | async-start | bytes 11796480 | tf_op jit(solution)/shard_map/all_gather | solution.py:47
  58.6 4.2 copy-start.5
  58.6 5.4 %copy-start = (bf16[3,128,4096]{2,1,0:T(8,128)(2,1)S(1)}, bf16[3,128,4096]{2,1,0:T(8,128)(2,1)}, u32[]{:S(2)}) copy-start(bf16[3,128,4096]{2,1,0:T(8,128)(2,1)} %param.9) | copy-start | bytes 9437188
  59.8 273.5 %all-gather.6.cloned.1.call-start = ((), (), s32[]{:S(2)}) async-start(), calls=%async_computation.2 | async-start | bytes 9437184 | tf_op jit(solution)/shard_map/all_gather | solution.py:45
  60.5 398.1 %all-gather.8.cloned.1.call-start = ((), (), s32[]{:S(2)}) async-start(), calls=%async_computation.4 | async-start | bytes 9437184 | tf_op jit(solution)/shard_map/all_gather | solution.py:46
  61.3 413.6 %reduce-scatter.3.cloned.1.call-start = ((), (), s32[]{:S(2)}) async-start(), calls=%async_computation.3 | async-start | bytes 2359296 | tf_op jit(solution)/shard_map/reduce_scatter | solution.py:78
  208.0 10.0 %copy-start.4 = (f32[4096]{0:T(1024)S(1)}, f32[4096]{0:T(1024)}, u32[]{:S(2)}) copy-start(f32[4096]{0:T(1024)} %param.14) | copy-start | bytes 49156
  333.3 125.3 %copy-start.2 = (bf16[3,128,4096]{2,1,0:T(8,128)(2,1)S(1)}, bf16[3,128,4096]{2,1,0:T(8,128)(2,1)}, u32[]{:S(2)}) copy-start(bf16[3,128,4096]{2,1,0:T(8,128)(2,1)} %multiply_convert_fusion) | copy-start | bytes 9437188
  342.4 138.1 %reduce-scatter.5.cloned.1.call-start = ((), (), s32[]{:S(2)}) async-start(), calls=%async_computation.5 | async-start | bytes 2359296 | tf_op jit(solution)/shard_map/reduce_scatter | solution.py:79
  465.6 8.0 %copy-start.1 = (f32[80,4096]{1,0:T(8,128)S(1)}, f32[80,4096]{1,0:T(8,128)}, u32[]{:S(2)}) copy-start(f32[80,4096]{1,0:T(8,128)} %reduce_sum.96) | copy-start | bytes 3932164
Sparse Core Ops, SparseCore 0:
  59.9 148.0 all-gather.9
  210.2 123.1 all-gather.5
  335.4 123.1 all-gather.7
  460.7 7.2 reduce-scatter.2
  470.1 10.2 reduce-scatter.4
